TPU v7x, 128 devices: a whole 4x4x4 slice. The times are simulated.
128 devices in a mesh: dp: 16 (over y, z), mp: 8 (over x, core).
Axes of the slice: x: 4, y: 4, z: 4, core: 2. Of those that a mesh axis runs over, the one named last changes fastest.
Arguments:
- grad_out: bfloat16 [16384, 6144], P(('dp', 'mp')), may hold values from -40 to 40
- context: bfloat16 [16384, 6144], P('dp', 'mp'), may hold values from -47 to 47
- weight: bfloat16 [6144, 6144], P(None, 'mp'), may hold values from -0.078125 to 0.078125
- master: float32 [6144, 6144], P('dp', 'mp'), may hold values from -0.6 to 0.6
- moment_q: bfloat16 [6144, 6144], P('dp', 'mp'), may hold values from -440 to 440
- second_moment: float32 [6144, 6144], P('dp', 'mp'), may hold values from 0.02 to 1
- moment_scale: float32 [], replicated, may hold values from 300 to 900
- scale_boost: float32 [], replicated, may hold values from 1.25 to 2
Outputs:
- input_grad: bfloat16 [16384, 6144], P('dp', 'mp')
- new_master: float32 [6144, 6144], P('dp', 'mp')
- new_moment_q: bfloat16 [6144, 6144], P('dp', 'mp')
- new_second: float32 [6144, 6144], P('dp', 'mp')
- new_scale: float32 [], replicated
- grad_scale: float32 [], replicated
- new_weight: bfloat16 [6144, 6144], P(None, 'mp')
All inputs are finite; a program needn't handle non-finite values. Where the computation divides by a largest or mean magnitude, that divisor is 1e-20 or more.
Results may differ from a plain program's by a relative error of at most 0.014.
Values may be sent and summed in bfloat16 or wider, within the bound.
No kernel may reach another device: no remote copies, remote signals or barrier semaphores. Data moves between devices by JAX's collectives and lax.ppermute only.
A program may use at most 128 MiB of HBM per device.

v0:
```python
import math
import jax
import jax.numpy as jnp
from jax import lax
from jax.sharding import PartitionSpec as P

D = 6144
HD = 6144
quant_top = 448.0
peak_eps = 1e-06
norm_eps = 1e-06
clip_rms = 0.5
beta_one = 0.9
beta_two = 0.95
bias_one = 1.0 - 0.9**10
bias_two = 1.0 - 0.95**10
adam_eps = 1e-08
rate_value = 0.01
decay_value = 0.1
contract_rows = (((0,), (0,)), ((), ()))


def input_product(full_grad, weight):
    return jnp.dot(full_grad, weight, preferred_element_type=jnp.float32).astype(jnp.bfloat16)


def weight_gradient(full_grad, context, scale_boost):
    held = lax.dot_general(full_grad, context, contract_rows, preferred_element_type=jnp.float32)
    local_peak = jnp.max(jnp.abs(held))
    peak = lax.pmax(local_peak, ("dp", "mp"))
    grad_scale = quant_top * scale_boost / (peak + peak_eps)
    scaled = held * grad_scale
    summed = lax.psum_scatter(
        jnp.clip(scaled, -quant_top, quant_top).astype(jnp.bfloat16),
        "dp",
        scatter_dimension=0,
        tiled=True,
    ).astype(jnp.float32)
    return (summed, grad_scale)


def local(grad_out, context, weight, master, moment_q, second_moment, moment_scale, scale_boost):
    full_grad = lax.all_gather(grad_out, "mp", axis=0, tiled=True)
    input_grad = input_product(full_grad, weight)
    summed, grad_scale = weight_gradient(full_grad, context, scale_boost)
    gradient = summed / grad_scale
    squares = lax.psum(jnp.sum(gradient * gradient), ("dp", "mp"))
    norm_value = jnp.sqrt(squares + norm_eps)
    clip_factor = clip_rms * math.sqrt(D * HD) / norm_value
    step_grad = clip_factor * gradient
    old_moment = moment_q.astype(jnp.float32) / moment_scale
    moment = beta_one * old_moment + (1.0 - beta_one) * step_grad
    new_second = beta_two * second_moment + (1.0 - beta_two) * step_grad * step_grad
    update = moment / bias_one / (jnp.sqrt(new_second / bias_two) + adam_eps) + decay_value * master
    new_master = master - rate_value * update
    moment_top = lax.pmax(jnp.max(jnp.abs(moment)), ("dp", "mp"))
    new_scale = quant_top / (moment_top + peak_eps)
    new_moment_q = (moment * new_scale).astype(jnp.bfloat16)
    new_weight = lax.all_gather(new_master.astype(jnp.bfloat16), "dp", axis=0, tiled=True)
    return (input_grad, new_master, new_moment_q, new_second, new_scale, grad_scale, new_weight)


def solution(mesh):
    return jax.shard_map(
        local,
        mesh=mesh,
        in_specs=(
            P(("dp", "mp"), None),
            P("dp", "mp"),
            P(None, "mp"),
            P("dp", "mp"),
            P("dp", "mp"),
            P("dp", "mp"),
            P(),
            P(),
        ),
        out_specs=(
            P("dp", "mp"),
            P("dp", "mp"),
            P("dp", "mp"),
            P("dp", "mp"),
            P(),
            P(),
            P(None, "mp"),
        ),
        check_vma=False,
    )
```

profile of v0, /device:TPU:1, one launch (start us, length us, event | category | flops | bytes accessed | tf_op | source)
XLA Modules:
  0.0 430.7 jit_solution(13931755045824228183)
XLA Ops:
  7.2 0.0 copy-start
  7.2 0.0 all-gather.3.cloned.1.call-start
  7.2 0.7 all-gather.3.cloned.1.call-update
  7.9 0.0 reduce-scatter.2.cloned.1.call-start
  8.6 72.1 %all-gather.3.cloned.1.call-done = bf16[1024,6144]{1,0:T(8,128)(2,1)} async-done(((bf16[128,6144]{1,0:T(8,128)(2,1)}), bf16[1024,6144]{1,0:T(8,128)(2,1)}) %all-gather.3.cloned.1.call-update) | async-done | bytes 12582928 | tf_op jit(solution)/shard_map/all_gather | solution.py:43
  80.7 0.0 copy-done
  80.7 17.7 %abs_reduce_fusion = (f32[]{:T(128)}, f32[6144,768]{1,0:T(8,128)}) fusion(bf16[1024,6144]{1,0:T(8,128)(2,1)} %all-gather.3.cloned.1.call-done, bf16[1024,768]{1,0:T(8,128)(2,1)S(1)} %copy-done), kind=kOutput, calls=%fused_computation.1 | convolution fusion | flops 9673113600 | bytes 33030148 | tf_op jit(solution)/shard_map/dot_general | solution.py:28
  98.3 64.9 %pmax.14 = f32[]{:T(128)} all-reduce(f32[]{:T(128)} %get-tuple-element.11), channel_id=1, replica_groups=mesh['dp'=16,'mp'=8] {'dp','mp'}, use_global_device_ids=true, to_apply=%region_1.0 | all-reduce | flops 1 | bytes 8 | tf_op jit(solution)/shard_map/pmax | solution.py:30
  164.0 11.6 %clamp_convert_fusion = bf16[6144,768]{1,0:T(8,128)(2,1)} fusion(f32[6144,768]{1,0:T(8,128)} %get-tuple-element.12, f32[]{:T(128)} %div.38), kind=kLoop, calls=%fused_computation | loop fusion | flops 14155776 | bytes 28311556 | tf_op jit(solution)/shard_map/convert_element_type | solution.py:34
  175.5 0.0 copy-start.2
  175.5 0.0 copy-start.3
  175.5 0.0 reduce-scatter.2.cloned.1.call-update
  175.5 0.0 all-gather.5.cloned.1.call-start
  175.6 83.8 %reduce-scatter.2.cloned.1.call-done = bf16[384,768]{1,0:T(8,128)(2,1)} async-done(((bf16[6144,768]{1,0:T(8,128)(2,1)}), bf16[384,768]{1,0:T(8,128)(2,1)}) %reduce-scatter.2.cloned.1.call-update) | async-done | bytes 589840 | tf_op jit(solution)/shard_map/reduce_scatter | solution.py:33
  259.4 2.0 multiply_reduce_fusion
  262.0 65.6 %psum.7 = f32[]{:T(128)} all-reduce(f32[]{:T(128)} %multiply_reduce_fusion), channel_id=1, replica_groups=mesh['dp'=16,'mp'=8] {'dp','mp'}, use_global_device_ids=true, to_apply=%region_4.5 | all-reduce | flops 1 | bytes 8 | tf_op jit(solution)/shard_map/psum | solution.py:47
  328.3 0.0 copy-done.2
  328.3 0.0 copy-done.3
  328.3 4.1 fusion.1
  332.4 0.0 all-gather.5.cloned.1.call-update
  332.5 0.7 abs_reduce_fusion.1
  333.1 15.6 %convolution_convert_fusion = bf16[1024,768]{1,0:T(8,128)(2,1)} fusion(bf16[1024,6144]{1,0:T(8,128)(2,1)} %all-gather.3.cloned.1.call-done, bf16[6144,768]{1,0:T(8,128)(2,1)} %param.10), kind=kOutput, calls=%fused_computation.3 | convolution fusion | flops 9664462848 | bytes 23592960 | tf_op jit(solution)/shard_map/dot_general | solution.py:24
  348.8 63.4 %pmax.15 = f32[]{:T(128)} all-reduce(f32[]{:T(128)} %abs_reduce_fusion.1), channel_id=1, replica_groups=mesh['dp'=16,'mp'=8] {'dp','mp'}, use_global_device_ids=true, to_apply=%region_6.7 | all-reduce | flops 1 | bytes 8 | tf_op jit(solution)/shard_map/pmax | solution.py:56
  412.9 0.9 multiply_convert_fusion
  413.8 0.0 all-gather.5.cloned.1.call-done
  413.8 0.0 copy-start.1
  413.8 8.1 %copy.18 = bf16[6144,768]{1,0:T(8,128)(2,1)} copy(bf16[6144,768]{1,0:T(8,128)(2,1)} %all-gather.5.cloned.1.call-done) | data formatting | bytes 18874368
  421.9 0.0 copy-done.1
Async XLA Ops:
  7.2 73.5 %copy-start = (bf16[1024,768]{1,0:T(8,128)(2,1)S(1)}, bf16[1024,768]{1,0:T(8,128)(2,1)}, u32[]{:S(2)}) copy-start(bf16[1024,768]{1,0:T(8,128)(2,1)} %param.9) | copy-start | bytes 4718596
  7.2 73.5 %all-gather.3.cloned.1.call-start = ((), (), s32[]{:S(2)}) async-start(), calls=%async_computation.1 | async-start | bytes 14155776 | tf_op jit(solution)/shard_map/all_gather | solution.py:43
  7.9 251.5 %reduce-scatter.2.cloned.1.call-start = ((), (), s32[]{:S(2)}) async-start(), calls=%async_computation.2 | async-start | bytes 10027008 | tf_op jit(solution)/shard_map/reduce_scatter | solution.py:33
  175.5 152.8 %copy-start.2 = (f32[384,768]{1,0:T(8,128)S(1)}, f32[384,768]{1,0:T(8,128)}, u32[]{:S(2)}) copy-start(f32[384,768]{1,0:T(8,128)} %param.11) | copy-start | bytes 3538948
  175.5 152.8 %copy-start.3 = (bf16[384,768]{1,0:T(8,128)(2,1)S(1)}, bf16[384,768]{1,0:T(8,128)(2,1)}, u32[]{:S(2)}) copy-start(bf16[384,768]{1,0:T(8,128)(2,1)} %param.12) | copy-start | bytes 1769476
  175.5 238.2 %all-gather.5.cloned.1.call-start = ((), (), s32[]{:S(2)}) async-start(), calls=%async_computation.3 | async-start | bytes 10027008 | tf_op jit(solution)/shard_map/all_gather | solution.py:59
  413.8 8.2 %copy-start.1 = (bf16[1024,768]{1,0:T(8,128)(2,1)S(1)}, bf16[1024,768]{1,0:T(8,128)(2,1)}, u32[]{:S(2)}) copy-start(bf16[1024,768]{1,0:T(8,128)(2,1)} %param.9) | copy-start | bytes 4718596
Sparse Core Ops, SparseCore 0:
  9.7 70.9 all-gather.2
  175.7 83.6 reduce-scatter.1
  332.6 72.7 all-gather.4
where the time goes:
time: 431 us
  blocking collectives  194 us (45%)
  waiting for transfers between devices  157 us (36%)
  matrix products  33.3 us (8%)
  between operations  19.4 us (5%)
  other arithmetic  19.2 us (4%)
  local copies, waits for them, and re-layouts  8.17 us (2%)
    reduce_scatter x1, waiting for transfers between devices, weight_gradient(): lax.psum_scatter(jnp.clip(scaled, -quant_top, quant_top).astype(jnp.bfloa...  83.8 us
    all_gather x1, waiting for transfers between devices, local(): full_grad = lax.all_gather(grad_out, 'mp', axis=0, tiled=True)  72.1 us
    psum x1, blocking collectives, local(): squares = lax.psum(jnp.sum(gradient * gradient), ('dp', 'mp'))  65.6 us
    pmax x1, blocking collectives, weight_gradient(): peak = lax.pmax(local_peak, ('dp', 'mp'))  64.9 us
    pmax x1, blocking collectives, local(): moment_top = lax.pmax(jnp.max(jnp.abs(moment)), ('dp', 'mp'))  63.4 us
    dot_general x1, matrix products, weight_gradient(): lax.dot_general(full_grad, context, contract_rows, preferred_element_type...  17.7 us
    dot_general x1, matrix products, input_product(): jnp.dot(full_grad, weight, preferred_element_type=jnp.float32)  15.6 us
    convert_element_type x1, other arithmetic, weight_gradient(): jnp.clip(scaled, -quant_top, quant_top).astype(jnp.bfloat16)  11.6 us
  transfers between devices with their start and end apart: 3, of which 2 were waited for; matrix products, arithmetic and copies ran while one was open for 4% of the time, Pallas kernels for 0%

commit v1 on v0

--- a/solution.py
+++ b/solution.py
@@ -40,7 +40,9 @@
 
 
 def local(grad_out, context, weight, master, moment_q, second_moment, moment_scale, scale_boost):
-    full_grad = lax.all_gather(grad_out, "mp", axis=0, tiled=True)
+    full_grad = jnp.concatenate(
+        lax.all_to_all(jnp.stack([grad_out] * lax.axis_size("mp")), "mp", 0, 0), axis=0
+    )
     input_grad = input_product(full_grad, weight)
     summed, grad_scale = weight_gradient(full_grad, context, scale_boost)
     gradient = summed / grad_scale

time: 431 us -> 513 us (1.19)
  waiting for transfers between devices: 157 us -> 222 us
  local copies, waits for them, and re-layouts: 8.17 us -> 15.8 us
  starting transfers between devices: 0.12 us -> 6.69 us
    all_to_all x0 -> x1, waiting for transfers between devices: none -> 138 us  [local(): lax.all_to_all(jnp.stack([grad_out] * lax.axis_size('mp')), 'mp', 0, 0)]
    all_gather x1 -> x0, waiting for transfers between devices: 72.1 us -> none  [local(): full_grad = lax.all_gather(grad_out, 'mp', axis=0, tiled=True)]
    another operation x0 -> x1, local copies, waits for them, and re-layouts: none -> 7.67 us  [local(): jnp.stack([grad_out] * lax.axis_size('mp'))]
    all_to_all x0 -> x1, starting transfers between devices: none -> 6.64 us  [local(): lax.all_to_all(jnp.stack([grad_out] * lax.axis_size('mp')), 'mp', 0, 0)]
  transfers between devices with their start and end apart: 3 -> 3, of which waited for: 2 -> 2; matrix products, arithmetic and copies ran while one was open for 4% -> 3% of each run, Pallas kernels for 0% -> 0%
where the time goes in v1:
time: 513 us; the launch traced here: 512 us
  waiting for transfers between devices  222 us (43%)
  blocking collectives  195 us (38%)
  matrix products  33.3 us (6%)
  between operations  19.7 us (4%)
  other arithmetic  19.2 us (4%)
  local copies, waits for them, and re-layouts  15.8 us (3%)
  starting transfers between devices  6.69 us (1%)
    all_to_all x1, waiting for transfers between devices, local(): lax.all_to_all(jnp.stack([grad_out] * lax.axis_size('mp')), 'mp', 0, 0)  138 us
    reduce_scatter x1, waiting for transfers between devices, weight_gradient(): lax.psum_scatter(jnp.clip(scaled, -quant_top, quant_top).astype(jnp.bfloa...  83.8 us
    pmax x1, blocking collectives, weight_gradient(): peak = lax.pmax(local_peak, ('dp', 'mp'))  66.5 us
    psum x1, blocking collectives, local(): squares = lax.psum(jnp.sum(gradient * gradient), ('dp', 'mp'))  65.4 us
    pmax x1, blocking collectives, local(): moment_top = lax.pmax(jnp.max(jnp.abs(moment)), ('dp', 'mp'))  63.5 us
    dot_general x1, matrix products, weight_gradient(): lax.dot_general(full_grad, context, contract_rows, preferred_element_type...  17.7 us
    dot_general x1, matrix products, input_product(): jnp.dot(full_grad, weight, preferred_element_type=jnp.float32)  15.6 us
    convert_element_type x1, other arithmetic, weight_gradient(): jnp.clip(scaled, -quant_top, quant_top).astype(jnp.bfloat16)  11.6 us
  transfers between devices with their start and end apart: 3, of which 2 were waited for; matrix products, arithmetic and copies ran while one was open for 3% of the time, Pallas kernels for 0%

profile of v1, /device:TPU:1, one launch (start us, length us, event | category | flops | bytes accessed | tf_op | source)
XLA Modules:
  0.0 512.2 jit_solution(12556564231941878470)
XLA Ops:
  7.2 0.0 copy-start
  7.2 7.7 %stack.2 = bf16[8,128,6144]{2,1,0:T(8,128)(2,1)} broadcast(bf16[128,6144]{1,0:T(8,128)(2,1)} %param.8), dimensions={1,2} | broadcast | bytes 14155776 | tf_op jit(solution)/shard_map/stack | solution.py:44
  14.8 6.6 %all-to-all-start = ((bf16[8,128,6144]{2,1,0:T(8,128)(2,1)}), bf16[8,128,6144]{2,1,0:T(8,128)(2,1)}, u32[]{:S(2)}, u32[]{:S(2)}) async-start(bf16[8,128,6144]{2,1,0:T(8,128)(2,1)} %stack.2), calls=%async_computation | async-start | bytes 25165824 | tf_op jit(solution)/shard_map/all_to_all | solution.py:44
  21.5 0.0 reduce-scatter.2.cloned.1.call-start
  22.1 138.2 %all-to-all-done = bf16[8,128,6144]{2,1,0:T(8,128)(2,1)} async-done(((bf16[8,128,6144]{2,1,0:T(8,128)(2,1)}), bf16[8,128,6144]{2,1,0:T(8,128)(2,1)}, u32[]{:S(2)}, u32[]{:S(2)}) %all-to-all-start) | async-done | bytes 12582944 | tf_op jit(solution)/shard_map/all_to_all | solution.py:44
  160.3 0.0 copy-done
  160.3 17.7 %abs_reduce_fusion = (f32[]{:T(128)}, f32[6144,768]{1,0:T(8,128)}) fusion(bf16[1024,6144]{1,0:T(8,128)(2,1)} %bitcast, bf16[1024,768]{1,0:T(8,128)(2,1)S(1)} %copy-done), kind=kOutput, calls=%fused_computation.1 | convolution fusion | flops 9673113600 | bytes 33030148 | tf_op jit(solution)/shard_map/dot_general | solution.py:28
  178.0 66.5 %pmax.14 = f32[]{:T(128)} all-reduce(f32[]{:T(128)} %get-tuple-element.11), channel_id=1, replica_groups=mesh['dp'=16,'mp'=8] {'dp','mp'}, use_global_device_ids=true, to_apply=%region_1.0 | all-reduce | flops 1 | bytes 8 | tf_op jit(solution)/shard_map/pmax | solution.py:30
  245.2 11.6 %clamp_convert_fusion = bf16[6144,768]{1,0:T(8,128)(2,1)} fusion(f32[6144,768]{1,0:T(8,128)} %get-tuple-element.12, f32[]{:T(128)} %div.38), kind=kLoop, calls=%fused_computation | loop fusion | flops 14155776 | bytes 28311556 | tf_op jit(solution)/shard_map/convert_element_type | solution.py:34
  256.7 0.0 copy-start.2
  256.7 0.0 copy-start.3
  256.7 0.0 reduce-scatter.2.cloned.1.call-update
  256.8 0.0 all-gather.2.cloned.1.call-start
  256.8 83.8 %reduce-scatter.2.cloned.1.call-done = bf16[384,768]{1,0:T(8,128)(2,1)} async-done(((bf16[6144,768]{1,0:T(8,128)(2,1)}), bf16[384,768]{1,0:T(8,128)(2,1)}) %reduce-scatter.2.cloned.1.call-update) | async-done | bytes 589840 | tf_op jit(solution)/shard_map/reduce_scatter | solution.py:33
  340.6 2.0 multiply_reduce_fusion
  343.2 65.4 %psum.7 = f32[]{:T(128)} all-reduce(f32[]{:T(128)} %multiply_reduce_fusion), channel_id=1, replica_groups=mesh['dp'=16,'mp'=8] {'dp','mp'}, use_global_device_ids=true, to_apply=%region_4.5 | all-reduce | flops 1 | bytes 8 | tf_op jit(solution)/shard_map/psum | solution.py:49
  409.3 0.0 copy-done.2
  409.4 0.0 copy-done.3
  409.4 4.1 fusion.1
  413.5 0.0 all-gather.2.cloned.1.call-update
  413.5 0.7 abs_reduce_fusion.1
  414.2 15.6 %convolution_convert_fusion = bf16[1024,768]{1,0:T(8,128)(2,1)} fusion(bf16[1024,6144]{1,0:T(8,128)(2,1)} %bitcast, bf16[6144,768]{1,0:T(8,128)(2,1)} %param.10), kind=kOutput, calls=%fused_computation.3 | convolution fusion | flops 9664462848 | bytes 23592960 | tf_op jit(solution)/shard_map/dot_general | solution.py:24
  429.8 63.5 %pmax.15 = f32[]{:T(128)} all-reduce(f32[]{:T(128)} %abs_reduce_fusion.1), channel_id=1, replica_groups=mesh['dp'=16,'mp'=8] {'dp','mp'}, use_global_device_ids=true, to_apply=%region_6.7 | all-reduce | flops 1 | bytes 8 | tf_op jit(solution)/shard_map/pmax | solution.py:58
  494.0 0.9 multiply_convert_fusion
  494.9 0.0 all-gather.2.cloned.1.call-done
  494.9 0.0 copy-start.1
  494.9 8.1 %copy.18 = bf16[6144,768]{1,0:T(8,128)(2,1)} copy(bf16[6144,768]{1,0:T(8,128)(2,1)} %all-gather.2.cloned.1.call-done) | data formatting | bytes 18874368
  503.1 0.0 copy-done.1
Async XLA Ops:
  7.2 153.1 %copy-start = (bf16[1024,768]{1,0:T(8,128)(2,1)S(1)}, bf16[1024,768]{1,0:T(8,128)(2,1)}, u32[]{:S(2)}) copy-start(bf16[1024,768]{1,0:T(8,128)(2,1)} %param.9) | copy-start | bytes 4718596
  14.8 145.5 %all-to-all-start = ((bf16[8,128,6144]{2,1,0:T(8,128)(2,1)}), bf16[8,128,6144]{2,1,0:T(8,128)(2,1)}, u32[]{:S(2)}, u32[]{:S(2)}) async-start(bf16[8,128,6144]{2,1,0:T(8,128)(2,1)} %stack.2), calls=%async_computation | async-start | bytes 25165824 | tf_op jit(solution)/shard_map/all_to_all | solution.py:44
  21.5 319.1 %reduce-scatter.2.cloned.1.call-start = ((), (), s32[]{:S(2)}) async-start(), calls=%async_computation.2 | async-start | bytes 10027008 | tf_op jit(solution)/shard_map/reduce_scatter | solution.py:33
  256.7 152.6 %copy-start.2 = (f32[384,768]{1,0:T(8,128)S(1)}, f32[384,768]{1,0:T(8,128)}, u32[]{:S(2)}) copy-start(f32[384,768]{1,0:T(8,128)} %param.11) | copy-start | bytes 3538948
  256.7 152.6 %copy-start.3 = (bf16[384,768]{1,0:T(8,128)(2,1)S(1)}, bf16[384,768]{1,0:T(8,128)(2,1)}, u32[]{:S(2)}) copy-start(bf16[384,768]{1,0:T(8,128)(2,1)} %param.12) | copy-start | bytes 1769476
  256.8 238.2 %all-gather.2.cloned.1.call-start = ((), (), s32[]{:S(2)}) async-start(), calls=%async_computation.3 | async-start | bytes 10027008 | tf_op jit(solution)/shard_map/all_gather | solution.py:61
  494.9 8.2 %copy-start.1 = (bf16[1024,768]{1,0:T(8,128)(2,1)S(1)}, bf16[1024,768]{1,0:T(8,128)(2,1)}, u32[]{:S(2)}) copy-start(bf16[1024,768]{1,0:T(8,128)(2,1)} %param.9) | copy-start | bytes 4718596
Sparse Core Ops, SparseCore 0:
  256.9 83.6 reduce-scatter.1
  413.6 72.8 all-gather.1
